TPU v7x, 32 devices: a whole 2x2x4 slice. The times are simulated.
32 devices in a mesh: grid: 8 (over y, x, core), ipts: 4 (over z).
Axes of the slice: x: 2, y: 2, z: 4, core: 2. Of those that a mesh axis runs over, the one named last changes fastest.
Arguments:
- orbitals: bfloat16 [16384, 1024], P(('grid', 'ipts')), may hold values from -1.1953125 to 1.1953125
- targets: bfloat16 [16384, 256], P(('grid', 'ipts')), may hold values from -6 to 6
- points: int32 [4, 1024], P('ipts', 'grid'), may hold values from 0 to 16383, as said below
- potential: bfloat16 [16384, 4096], P('grid', 'ipts'), may hold values from -0.09375 to 0.09375
Outputs:
- exchanged: bfloat16 [16384, 256], P(('grid', 'ipts'))
Inputs may be any that keep to these rules, and one draw needn't show every extreme that they name: Indices are distinct over all groups; each row of points rises strictly, and its entries k * 128 to (k + 1) * 128 - 1 lie in grid rows k * 2048 to (k + 1) * 2048 - 1.
All inputs are finite; a program needn't handle non-finite values.
Results may differ from a plain program's by a relative error of at most 0.0049.
Values may be sent and summed in bfloat16 or wider, within the bound.
A program may use at most 128 MiB of HBM per device.

v0:
```python
import jax
import jax.numpy as jnp
from jax import lax
from jax.sharding import PartitionSpec as P


def local(orbitals, targets, points, potential):
    groups = lax.axis_size("ipts")
    own_rows = orbitals.shape[0]
    slab_length = own_rows * groups
    slab_start = lax.axis_index("grid") * slab_length
    whole_slab = lax.all_gather(orbitals, "ipts", axis=0, tiled=True)
    every_group = lax.all_gather(points, "ipts", axis=0, tiled=True)
    orbital_values = jnp.take(whole_slab, points[0] - slab_start, axis=0)
    offset = every_group - (slab_start + lax.axis_index("ipts") * own_rows)
    inside = (offset >= 0) & (offset < own_rows)
    clipped = jnp.clip(offset, 0, own_rows - 1)
    picked = jnp.take(targets, clipped, axis=0) * inside[:, :, None].astype(targets.dtype)
    summed = lax.psum_scatter(picked, "ipts", scatter_dimension=0, tiled=True).astype(jnp.float32)
    target_values = summed[0].astype(jnp.bfloat16)
    orbital_piece = lax.all_gather(orbital_values, "grid", axis=0, tiled=True)
    target_piece = lax.all_gather(target_values, "grid", axis=0, tiled=True)
    products = lax.dot_general(
        whole_slab, orbital_piece, (((1,), (1,)), ((), ())), preferred_element_type=jnp.float32
    )
    weighted = (potential * products).astype(jnp.bfloat16)
    group_total = jnp.dot(weighted, target_piece, preferred_element_type=jnp.float32)
    summed_rows = lax.psum_scatter(group_total, "ipts", scatter_dimension=0, tiled=True)
    return (-summed_rows).astype(jnp.bfloat16)


def solution(mesh):
    placed = (
        P(("grid", "ipts"), None),
        P(("grid", "ipts"), None),
        P("ipts", "grid"),
        P("grid", "ipts"),
    )
    return jax.shard_map(
        local, mesh=mesh, in_specs=placed, out_specs=P(("grid", "ipts"), None), check_vma=False
    )
```

profile of v0, /device:TPU:0, one launch (start us, length us, event | category | flops | bytes accessed | tf_op | source)
XLA Modules:
  0.0 204.3 jit_solution(11490571779918535644)
XLA Ops:
  6.5 0.0 copy-start
  6.5 0.0 all-gather.5.cloned.1.call-start
  6.5 0.7 all-gather.5.cloned.1.call-update
  7.3 0.0 reduce-scatter.3.cloned.1.call-start
  7.3 12.8 %all-gather.1 = s32[4,1,128]{2,1,0:T(1,128)S(1)} all-gather(s32[1,1,128]{2,1,0:T(1,128)} %bitcast.29), channel_id=1, replica_groups=mesh['grid'=8,'ipts'=4] {'ipts'}, dimensions={0}, use_global_device_ids=true | all-gather | bytes 2560 | tf_op jit(solution)/shard_map/all_gather | solution.py:13
  20.2 0.0 copy-done
  20.2 2.0 gather_fusion.1
  22.2 0.9 select_multiply_fusion
  23.1 0.0 reduce-scatter.3.cloned.1.call-update
  23.1 0.0 all-gather.7.cloned.1.call-start
  23.2 0.0 copy-done.1
  23.2 69.2 %all-gather.5.cloned.1.call-done = bf16[2048,1024]{1,0:T(8,128)(2,1)} async-done(((bf16[512,1024]{1,0:T(8,128)(2,1)}), bf16[2048,1024]{1,0:T(8,128)(2,1)}) %all-gather.5.cloned.1.call-update) | async-done | bytes 4194320 | tf_op jit(solution)/shard_map/all_gather | solution.py:12
  92.4 3.8 %gather_fusion = bf16[128,1024]{1,0:T(8,128)(2,1)S(1)} fusion(bf16[2048,1024]{1,0:T(8,128)(2,1)} %all-gather.5.cloned.1.call-done, s32[1024]{0:T(1024)S(1)} %pad_clamp_fusion.1), kind=kCustom, calls=%fused_computation | custom fusion | bytes 524800 | tf_op jit(solution)/shard_map/jit(_take)/gather | solution.py:14
  96.2 0.8 broadcast_select_fusion
  97.0 0.0 all-gather.7.cloned.1.call-update
  97.0 0.0 reduce-scatter.5.cloned.1.call-start
  97.0 6.5 %copy.5 = bf16[2048,1024]{0,1:T(8,128)(2,1)} copy(bf16[2048,1024]{1,0:T(8,128)(2,1)} %param.7) | data formatting | bytes 8388608 | tf_op args[3]
  103.6 9.6 %reduce-scatter.3.cloned.1.call-done = bf16[1,128,256]{2,1,0:T(8,128)(2,1)} async-done(((bf16[4,128,256]{2,1,0:T(8,128)(2,1)}), bf16[1,128,256]{2,1,0:T(8,128)(2,1)}) %reduce-scatter.3.cloned.1.call-update) | async-done | bytes 65552 | tf_op jit(solution)/shard_map/reduce_scatter | solution.py:19
  113.2 10.1 %all-gather = bf16[1,1024,256]{2,1,0:T(8,128)(2,1)S(1)} all-gather(bf16[1,128,256]{2,1,0:T(8,128)(2,1)} %reduce-scatter.3.cloned.1.call-done), channel_id=2, replica_groups=mesh['grid'=8,'ipts'=4] {'grid'}, dimensions={1}, use_global_device_ids=true | all-gather | bytes 589824 | tf_op jit(solution)/shard_map/all_gather | solution.py:22
  123.3 17.8 %all-gather.7.cloned.1.call-done = bf16[1024,1024]{1,0:T(8,128)(2,1)} async-done(((bf16[128,1024]{1,0:T(8,128)(2,1)}), bf16[1024,1024]{1,0:T(8,128)(2,1)}) %all-gather.7.cloned.1.call-update) | async-done | bytes 2097168 | tf_op jit(solution)/shard_map/all_gather | solution.py:21
  141.1 11.0 %fusion.1 = f32[2048,256]{1,0:T(8,128)} fusion(bf16[2048,1024]{0,1:T(8,128)(2,1)} %copy.5, bf16[1024,1024]{1,0:T(8,128)(2,1)} %all-gather.7.cloned.1.call-done, bf16[2048,1024]{1,0:T(8,128)(2,1)} %all-gather.5.cloned.1.call-done, bf16[1,1024,256]{2,1,0:T(8,128)(2,1)S(1)} %all-gather), kind=kOutput, calls=%fused_computation.4 | convolution fusion | flops 5375000576 | bytes 13107200 | tf_op jit(solution)/shard_map/dot_general | solution.py:27
  152.1 0.0 reduce-scatter.5.cloned.1.call-update
  152.2 43.8 %reduce-scatter.5.cloned.1.call-done = f32[512,256]{1,0:T(8,128)} async-done(((f32[2048,256]{1,0:T(8,128)}), f32[512,256]{1,0:T(8,128)}) %reduce-scatter.5.cloned.1.call-update) | async-done | bytes 524304 | tf_op jit(solution)/shard_map/reduce_scatter | solution.py:28
  195.9 1.8 negate_convert_fusion
  (10 shorter events, 0.1 us)
Async XLA Ops:
  6.5 13.6 %copy-start = (bf16[512,256]{1,0:T(8,128)(2,1)S(1)}, bf16[512,256]{1,0:T(8,128)(2,1)}, u32[]{:S(2)}) copy-start(bf16[512,256]{1,0:T(8,128)(2,1)} %param.5) | copy-start | bytes 786436
  6.5 16.6 %copy-start.1 = (s32[1,128]{1,0:T(1,128)S(1)}, s32[1,128]{1,0:T(1,128)}, u32[]{:S(2)}) copy-start(s32[1,128]{1,0:T(1,128)} %param.6) | copy-start | bytes 1540
  6.5 85.9 %all-gather.5.cloned.1.call-start = ((), (), s32[]{:S(2)}) async-start(), calls=%async_computation.2 | async-start | bytes 5242880 | tf_op jit(solution)/shard_map/all_gather | solution.py:12
  7.3 105.9 %reduce-scatter.3.cloned.1.call-start = ((), (), s32[]{:S(2)}) async-start(), calls=%async_computation.4 | async-start | bytes 327680 | tf_op jit(solution)/shard_map/reduce_scatter | solution.py:19
  23.1 118.0 %all-gather.7.cloned.1.call-start = ((), (), s32[]{:S(2)}) async-start(), calls=%async_computation.3 | async-start | bytes 2359296 | tf_op jit(solution)/shard_map/all_gather | solution.py:21
  97.0 98.9 %reduce-scatter.5.cloned.1.call-start = ((), (), s32[]{:S(2)}) async-start(), calls=%async_computation.5 | async-start | bytes 2621440 | tf_op jit(solution)/shard_map/reduce_scatter | solution.py:28
Sparse Core Ops, SparseCore 0:
  8.9 83.4 all-gather.4
  94.7 18.4 reduce-scatter.2
  115.1 25.9 all-gather.6
  152.3 43.6 reduce-scatter.4
where the time goes:
time: 205 us; the launch traced here: 204 us
  waiting for transfers between devices  141 us (69%)
  blocking collectives  22.9 us (11%)
  between operations  13.2 us (6%)
  local copies, waits for them, and re-layouts  12.3 us (6%)
  matrix products  11 us (5%)
  other arithmetic  3.55 us (2%)
    all_gather x1, waiting for transfers between devices, local(): whole_slab = lax.all_gather(orbitals, 'ipts', axis=0, tiled=True)  69.2 us
    reduce_scatter x1, waiting for transfers between devices, local(): lax.psum_scatter(group_total, 'ipts', scatter_dimension=0, tiled=True)  43.8 us
    all_gather x1, waiting for transfers between devices, local(): orbital_piece = lax.all_gather(orbital_values, 'grid', axis=0, tiled=True)  17.8 us
    all_gather x1, blocking collectives, local(): every_group = lax.all_gather(points, 'ipts', axis=0, tiled=True)  12.8 us
    dot_general x1, matrix products, local(): jnp.dot(weighted, target_piece, preferred_element_type=jnp.float32)  11 us
    all_gather x1, blocking collectives, local(): target_piece = lax.all_gather(target_values, 'grid', axis=0, tiled=True)  10.1 us
    reduce_scatter x1, waiting for transfers between devices, local(): lax.psum_scatter(picked, 'ipts', scatter_dimension=0, tiled=True)  9.59 us
    unnamed x6, local copies, waits for them, and re-layouts  6.53 us
  transfers between devices with their start and end apart: 4, of which 4 were waited for; matrix products, arithmetic and copies ran while one was open for 7% of the time, Pallas kernels for 0%

commit v1 on v0

--- a/solution.py
+++ b/solution.py
@@ -9,7 +9,12 @@
     own_rows = orbitals.shape[0]
     slab_length = own_rows * groups
     slab_start = lax.axis_index("grid") * slab_length
-    whole_slab = lax.all_gather(orbitals, "ipts", axis=0, tiled=True)
+    ring = [orbitals]
+    for hop in range(3):
+        ring.append(lax.ppermute(ring[-1], "ipts", [(dev, (dev + 1) % 4) for dev in range(4)]))
+    whole_slab = jnp.roll(
+        jnp.concatenate(ring[::-1], axis=0), (lax.axis_index("ipts") + 1) * ring[0].shape[0], axis=0
+    )
     every_group = lax.all_gather(points, "ipts", axis=0, tiled=True)
     orbital_values = jnp.take(whole_slab, points[0] - slab_start, axis=0)
     offset = every_group - (slab_start + lax.axis_index("ipts") * own_rows)

time: 205 us -> 193 us (0.941)
  waiting for transfers between devices: 141 us -> 105 us
  blocking collectives: 22.9 us -> 39 us
  starting transfers between devices: 0.12 us -> 5.03 us
  other arithmetic: 3.55 us -> 5.79 us
    all_gather x1 -> x0, waiting for transfers between devices: 69.2 us -> none  [local(): whole_slab = lax.all_gather(orbitals, 'ipts', axis=0, tiled=True)]
    ppermute x0 -> x3, waiting for transfers between devices: none -> 46.7 us  [local(): lax.ppermute(ring[-1], 'ipts', [(dev, (dev + 1) % 4) for dev in range(4)])]
    all_gather x1, blocking collectives: 12.8 us -> 28 us  [local(): every_group = lax.all_gather(points, 'ipts', axis=0, tiled=True)]
    reduce_scatter x1, waiting for transfers between devices: 9.59 us -> 0.02 us  [local(): lax.psum_scatter(picked, 'ipts', scatter_dimension=0, tiled=True)]
    ppermute x0 -> x3, starting transfers between devices: none -> 4.94 us  [local(): lax.ppermute(ring[-1], 'ipts', [(dev, (dev + 1) % 4) for dev in range(4)])]
    unnamed x6 -> x12, local copies, waits for them, and re-layouts: 6.53 us -> 2.95 us
    all_gather x1, waiting for transfers between devices: 17.8 us -> 14.5 us  [local(): orbital_piece = lax.all_gather(orbital_values, 'grid', axis=0, tiled=True)]
    dynamic_slice x0 -> x1, local copies, waits for them, and re-layouts: none -> 2.38 us  [local(): jnp.roll(jnp.concatenate(ring[::-1], axis=0), (lax.axis_index('ipts') + 1...]
  transfers between devices with their start and end apart: 4 -> 6, of which waited for: 4 -> 4; matrix products, arithmetic and copies ran while one was open for 7% -> 8% of each run, Pallas kernels for 0% -> 0%
where the time goes in v1:
time: 193 us
  waiting for transfers between devices  105 us (54%)
  blocking collectives  39 us (20%)
  between operations  15 us (8%)
  local copies, waits for them, and re-layouts  11.8 us (6%)
  matrix products  11.2 us (6%)
  other arithmetic  5.79 us (3%)
  starting transfers between devices  5.03 us (3%)
    ppermute x3, waiting for transfers between devices, local(): lax.ppermute(ring[-1], 'ipts', [(dev, (dev + 1) % 4) for dev in range(4)])  46.7 us
    reduce_scatter x1, waiting for transfers between devices, local(): lax.psum_scatter(group_total, 'ipts', scatter_dimension=0, tiled=True)  43.8 us
    all_gather x1, blocking collectives, local(): every_group = lax.all_gather(points, 'ipts', axis=0, tiled=True)  28 us
    all_gather x1, waiting for transfers between devices, local(): orbital_piece = lax.all_gather(orbital_values, 'grid', axis=0, tiled=True)  14.5 us
    dot_general x1, matrix products, local(): jnp.dot(weighted, target_piece, preferred_element_type=jnp.float32)  11.2 us
    all_gather x1, blocking collectives, local(): target_piece = lax.all_gather(target_values, 'grid', axis=0, tiled=True)  11.1 us
    ppermute x3, starting transfers between devices, local(): lax.ppermute(ring[-1], 'ipts', [(dev, (dev + 1) % 4) for dev in range(4)])  4.94 us
  transfers between devices with their start and end apart: 6, of which 4 were waited for; matrix products, arithmetic and copies ran while one was open for 8% of the time, Pallas kernels for 0%

profile of v1, /device:TPU:0, one launch (start us, length us, event | category | flops | bytes accessed | tf_op | source)
XLA Modules:
  0.0 192.8 jit_solution(12178539948833164961)
XLA Ops:
  7.4 3.1 %collective-permute-start = (bf16[512,1024]{1,0:T(8,128)(2,1)}, bf16[512,1024]{1,0:T(8,128)(2,1)S(1)}, u32[]{:S(2)}, u32[]{:S(2)}) collective-permute-start(bf16[512,1024]{1,0:T(8,128)(2,1)} %param.4), channel_id=1, source_target_pairs={{0,1},{1,2},{2,3},{3,0},{4,5},{5,6},{6,7},{7,4},{8,9},{9,10},{10,1... | collective-permute-start | bytes 3145736 | tf_op jit(solution)/shard_map/ppermute | solution.py:14
  10.4 25.4 %collective-permute-done = bf16[512,1024]{1,0:T(8,128)(2,1)S(1)} collective-permute-done((bf16[512,1024]{1,0:T(8,128)(2,1)}, bf16[512,1024]{1,0:T(8,128)(2,1)S(1)}, u32[]{:S(2)}, u32[]{:S(2)}) %collective-permute-start) | collective-permute-done | bytes 1048608 | tf_op jit(solution)/shard_map/ppermute | solution.py:14
  35.9 28.0 %all-gather.1 = s32[4,1,128]{2,1,0:T(1,128)S(1)} all-gather(s32[1,1,128]{2,1,0:T(1,128)} %bitcast.23), channel_id=1, replica_groups=mesh['grid'=8,'ipts'=4] {'ipts'}, dimensions={0}, use_global_device_ids=true | all-gather | bytes 2560 | tf_op jit(solution)/shard_map/all_gather | solution.py:18
  63.9 1.9 collective-permute-start.2
  65.8 2.6 %gather_fusion.1 = bf16[512,256]{1,0:T(8,128)(2,1)} fusion(bf16[512,256]{1,0:T(8,128)(2,1)S(1)} %copy-done, s32[1024]{0:T(1024)S(1)} %pad_clamp_fusion), kind=kCustom, calls=%fused_computation.1 | custom fusion | bytes 526336 | tf_op jit(solution)/shard_map/jit(_take)/gather | solution.py:23
  68.4 1.9 select_multiply_fusion
  70.3 0.7 fusion.3
  71.0 0.7 compare_and_fusion.1
  71.6 21.3 %collective-permute-done.2 = bf16[512,1024]{1,0:T(8,128)(2,1)} collective-permute-done((bf16[512,1024]{1,0:T(8,128)(2,1)S(1)}, bf16[512,1024]{1,0:T(8,128)(2,1)}, u32[]{:S(2)}, u32[]{:S(2)}) %collective-permute-start.2) | collective-permute-done | bytes 1048608 | tf_op jit(solution)/shard_map/ppermute | solution.py:14
  92.9 1.3 constant_dynamic-update-slice_fusion.7
  94.2 0.1 constant_dynamic-update-slice_fusion.6
  94.3 0.1 constant_dynamic-update-slice_fusion.5
  94.5 1.3 constant_dynamic-update-slice_fusion.3
  95.8 0.1 constant_dynamic-update-slice_fusion.2
  95.8 0.1 constant_dynamic-update-slice_fusion.1
  95.9 0.1 constant_dynamic-update-slice_fusion
  96.0 2.4 %constant_dynamic-slice_fusion = bf16[2048,1024]{1,0:T(8,128)(2,1)} fusion(bf16[4096,1024]{1,0:T(8,128)(2,1)S(1)} %constant_dynamic-update-slice_fusion, s32[]{:T(128)S(6)} %select_n.43), kind=kLoop, calls=%fused_computation.28 | loop fusion | bytes 8388612 | tf_op jit(solution)/shard_map/jit(_roll_dynamic)/dynamic_slice | solution.py:15
  98.4 3.8 %gather_fusion = bf16[128,1024]{1,0:T(8,128)(2,1)S(1)} fusion(bf16[2048,1024]{1,0:T(8,128)(2,1)} %constant_dynamic-slice_fusion, s32[1024]{0:T(1024)S(1)} %pad_clamp_fusion.1), kind=kCustom, calls=%fused_computation | custom fusion | bytes 524800 | tf_op jit(solution)/shard_map/jit(_take)/gather | solution.py:19
  102.1 0.8 broadcast_select_fusion
  103.0 11.1 %all-gather = bf16[1,1024,256]{2,1,0:T(8,128)(2,1)S(1)} all-gather(bf16[1,128,256]{2,1,0:T(8,128)(2,1)} %reduce-scatter.3.cloned.1.call-done), channel_id=2, replica_groups=mesh['grid'=8,'ipts'=4] {'grid'}, dimensions={1}, use_global_device_ids=true | all-gather | bytes 589824 | tf_op jit(solution)/shard_map/all_gather | solution.py:27
  114.1 14.5 %all-gather.4.cloned.1.call-done = bf16[1024,1024]{1,0:T(8,128)(2,1)} async-done(((bf16[128,1024]{1,0:T(8,128)(2,1)}), bf16[1024,1024]{1,0:T(8,128)(2,1)}) %all-gather.4.cloned.1.call-update) | async-done | bytes 2097168 | tf_op jit(solution)/shard_map/all_gather | solution.py:26
  128.6 11.2 %fusion = f32[2048,256]{1,0:T(8,128)} fusion(bf16[2048,1024]{1,0:T(8,128)(2,1)} %param.7, bf16[2048,1024]{1,0:T(8,128)(2,1)} %constant_dynamic-slice_fusion, bf16[1024,1024]{1,0:T(8,128)(2,1)} %all-gather.4.cloned.1.call-done, bf16[1,1024,256]{2,1,0:T(8,128)(2,1)S(1)} %all-gather), kind=kOutput, calls=%fused_computation.3 | convolution fusion | flops 5375000576 | bytes 13107200 | tf_op jit(solution)/shard_map/dot_general | solution.py:32
  139.8 43.8 %reduce-scatter.5.cloned.1.call-done = f32[512,256]{1,0:T(8,128)} async-done(((f32[2048,256]{1,0:T(8,128)}), f32[512,256]{1,0:T(8,128)}) %reduce-scatter.5.cloned.1.call-update) | async-done | bytes 524304 | tf_op jit(solution)/shard_map/reduce_scatter | solution.py:33
  183.6 1.8 negate_convert_fusion
  (21 shorter events, 0.3 us)
Async XLA Ops:
  7.4 58.4 %copy-start = (bf16[512,256]{1,0:T(8,128)(2,1)S(1)}, bf16[512,256]{1,0:T(8,128)(2,1)}, u32[]{:S(2)}) copy-start(bf16[512,256]{1,0:T(8,128)(2,1)} %param.5) | copy-start | bytes 786436
  7.4 87.0 %copy-start.1 = (bf16[512,1024]{1,0:T(8,128)(2,1)S(1)}, bf16[512,1024]{1,0:T(8,128)(2,1)}, u32[]{:S(2)}) copy-start(bf16[512,1024]{1,0:T(8,128)(2,1)} %param.4) | copy-start | bytes 3145732
  7.4 95.7 %reduce-scatter.3.cloned.1.call-start = ((), (), s32[]{:S(2)}) async-start(), calls=%async_computation.3 | async-start | bytes 327680 | tf_op jit(solution)/shard_map/reduce_scatter | solution.py:24
  7.4 28.5 %collective-permute-start = (bf16[512,1024]{1,0:T(8,128)(2,1)}, bf16[512,1024]{1,0:T(8,128)(2,1)S(1)}, u32[]{:S(2)}, u32[]{:S(2)}) collective-permute-start(bf16[512,1024]{1,0:T(8,128)(2,1)} %param.4), channel_id=1, source_target_pairs={{0,1},{1,2},{2,3},{3,0},{4,5},{5,6},{6,7},{7,4},{8,9},{9,10},{10,1... | collective-permute-start | bytes 3145736 | tf_op jit(solution)/shard_map/ppermute | solution.py:14
  35.8 28.0 %collective-permute-start.1 = (bf16[512,1024]{1,0:T(8,128)(2,1)S(1)}, bf16[512,1024]{1,0:T(8,128)(2,1)S(1)}, u32[]{:S(2)}, u32[]{:S(2)}) collective-permute-start(bf16[512,1024]{1,0:T(8,128)(2,1)S(1)} %collective-permute-done), channel_id=1, source_target_pairs={{0,1},{1,2},{2,3},{3,0},{4,5},{5,6},{6,7},{7,4},{8,9},{9,10},{10,1... | collective-permute-start | bytes 3145736 | tf_op jit(solution)/shard_map/ppermute | solution.py:14
  63.9 29.1 %collective-permute-start.2 = (bf16[512,1024]{1,0:T(8,128)(2,1)S(1)}, bf16[512,1024]{1,0:T(8,128)(2,1)}, u32[]{:S(2)}, u32[]{:S(2)}) collective-permute-start(bf16[512,1024]{1,0:T(8,128)(2,1)S(1)} %collective-permute-done.1), channel_id=1, source_target_pairs={{0,1},{1,2},{2,3},{3,0},{4,5},{5,6},{6,7},{7,4},{8,9},{9,10},{10,1... | collective-permute-start | bytes 3145736 | tf_op jit(solution)/shard_map/ppermute | solution.py:14
  70.2 58.3 %all-gather.4.cloned.1.call-start = ((), (), s32[]{:S(2)}) async-start(), calls=%async_computation.2 | async-start | bytes 2359296 | tf_op jit(solution)/shard_map/all_gather | solution.py:26
  103.0 80.6 %reduce-scatter.5.cloned.1.call-start = ((), (), s32[]{:S(2)}) async-start(), calls=%async_computation.4 | async-start | bytes 2621440 | tf_op jit(solution)/shard_map/reduce_scatter | solution.py:33
Sparse Core Ops, SparseCore 0:
  70.4 21.4 reduce-scatter.2
  139.9 43.6 reduce-scatter.4
Sparse Core Ops, SparseCore 1:
  103.1 25.5 all-gather.3
